TPU v7x, 256 devices: a whole 4x4x8 slice. The times are simulated.
256 devices in a mesh: query: 16 (over z, y_lo), db: 16 (over x, y_hi, core).
Axes of the slice: x: 4, y: 4 (y_hi: 2, y_lo: 2; y = y_hi * 2 + y_lo), z: 8, core: 2. Of those that a mesh axis runs over, the one named last changes fastest.
Arguments:
- noisy_images: float32 [16, 3, 128, 128], P('db', None, 'query'), may hold values from -6 to 6
- database: bfloat16 [432, 262144], P(None, 'db'), may hold values from -4 to 4
- picked_blocks: int32 [16, 4], P('db'), may hold values from 0 to 7, as said below
- alpha_now: float32 [16], replicated, may hold values from 0.15 to 0.35
- alpha_next: float32 [16], replicated, may hold values from 0.4 to 0.8
Outputs:
- next_images: float32 [16, 3, 128, 128], P('db', None, 'query')
Inputs may be any that keep to these rules, and one draw needn't show every extreme that they name: `picked_blocks`: each row names 4 different windows of the 8 stored on that shard.
All inputs are finite; a program needn't handle non-finite values.
Results may differ from a plain program's by a relative error of at most 0.00075.
Values may be sent and summed in bfloat16 or wider, within the bound.
A program may use at most 192 MiB of HBM per device.

v0:
```python
import jax
import jax.numpy as jnp
from jax import lax
from jax.sharding import PartitionSpec as P

BLOCK = 2048


def shifted(value, axis, by):
    count = lax.axis_size(axis)
    return lax.ppermute(value, axis, [(i, (i + by) % count) for i in range(count)])


def combined_all(value, axis, combine):
    everything = jax.tree.map(lambda part: lax.all_gather(part, axis), value)
    first = jax.tree.map(lambda part: part[0], everything)

    def lap(k, so_far):
        return combine(so_far, jax.tree.map(lambda part: part[k], everything))

    return lax.fori_loop(1, lax.axis_size(axis), lap, first)


def extract(pixels):
    height = pixels.shape[2] - 8
    across = pixels.shape[3] - 8
    slab_list = []
    for row_shift in range(12):
        for col_shift in range(12):
            slab_list.append(
                pixels[:, :, row_shift : row_shift + height : 4, col_shift : col_shift + across : 4]
            )
    stacked = jnp.stack(slab_list)
    stacked = stacked.reshape(12, 12, stacked.shape[1], 3, stacked.shape[3], stacked.shape[4])
    stacked = jnp.transpose(stacked, (3, 0, 1, 2, 4, 5))
    return stacked.reshape(432, -1)


def combine(first, second):
    top = jnp.maximum(first[0], second[0])
    factor_one = jnp.exp(first[0] - top)
    factor_two = jnp.exp(second[0] - top)
    totals = first[1] * factor_one + second[1] * factor_two
    numerator = first[2] * factor_one[None, :] + second[2] * factor_two[None, :]
    return (top, totals, numerator)


def on_device(noisy_images, database, picked_blocks, alpha_now, alpha_next):
    images_dev, channels, height, across = noisy_images.shape
    rounded = noisy_images.astype(jnp.bfloat16)
    below = shifted(rounded, "query", -1)
    extended = jnp.concatenate([rounded, below], axis=2)
    extended = jnp.concatenate([extended, extended[:, :, :, :8]], axis=3)
    per_image = height // 4 * (across // 4)
    gathered = lax.all_gather(extract(extended), "db", axis=1, tiled=True)
    count = gathered.shape[1]
    per_query = jnp.repeat(alpha_now, per_image)
    linear = jnp.sqrt(per_query) / (1.0 - per_query)
    quadratic = per_query / (2.0 * (1.0 - per_query))
    maxima = jnp.full((count,), -jnp.inf, jnp.float32)
    totals = jnp.zeros((count,), jnp.float32)
    numerator = jnp.zeros((432, count), jnp.float32)
    for slot in range(picked_blocks.shape[1]):
        offset = picked_blocks[0, slot] * BLOCK
        window = lax.dynamic_slice_in_dim(database, offset, BLOCK, 1)
        squares = jnp.sum(window.astype(jnp.float32) ** 2, axis=0)
        inner = lax.dot_general(
            gathered, window, (((0,), (0,)), ((), ())), preferred_element_type=jnp.float32
        )
        logits = linear[:, None] * inner - quadratic[:, None] * squares[None, :]
        new_max = jnp.maximum(maxima, jnp.max(logits, axis=1))
        rescale = jnp.exp(maxima - new_max)
        raw = jnp.exp(logits - new_max[:, None])
        totals = totals * rescale + jnp.sum(raw, axis=1)
        weighted = lax.dot_general(
            window,
            raw.astype(jnp.bfloat16),
            (((1,), (1,)), ((), ())),
            preferred_element_type=jnp.float32,
        )
        numerator = numerator * rescale[None, :] + weighted
        maxima = new_max
    per_device = images_dev * per_image
    maxima, totals, numerator = combined_all((maxima, totals, numerator), "db", combine)
    own_start = lax.axis_index("db") * per_device
    totals = lax.dynamic_slice_in_dim(totals, own_start, per_device, 0)
    numerator = lax.dynamic_slice_in_dim(numerator, own_start, per_device, 1)
    estimate = numerator / totals[None, :]
    pieces = estimate.reshape(3, 3, 4, 3, 4, images_dev, height // 4, across // 4)
    accum = jnp.zeros((images_dev, 3, height // 4 + 2, 4, across // 4 + 2, 4), jnp.float32)
    for coarse_row in range(3):
        for coarse_col in range(3):
            piece = jnp.transpose(pieces[:, coarse_row, :, coarse_col], (3, 0, 4, 1, 5, 2))
            accum = accum + jnp.pad(
                piece,
                (
                    (0, 0),
                    (0, 0),
                    (coarse_row, 2 - coarse_row),
                    (0, 0),
                    (coarse_col, 2 - coarse_col),
                    (0, 0),
                ),
            )
    summed = accum.reshape(images_dev, 3, height + 8, across + 8)
    summed = summed[:, :, :, :across].at[:, :, :, :8].add(summed[:, :, :, across:])
    spill = shifted(summed[:, :, height:, :], "query", 1)
    denoised = summed[:, :, :height, :].at[:, :, :8, :].add(spill) / 9.0
    own_images = lax.axis_index("db") * images_dev
    signal = lax.dynamic_slice_in_dim(alpha_now, own_images, images_dev, 0)[:, None, None, None]
    after = lax.dynamic_slice_in_dim(alpha_next, own_images, images_dev, 0)[:, None, None, None]
    noise_part = (noisy_images - jnp.sqrt(signal) * denoised) / jnp.sqrt(1.0 - signal)
    return jnp.sqrt(after) * denoised + jnp.sqrt(1.0 - after) * noise_part


def solution(mesh):
    return jax.shard_map(
        on_device,
        mesh=mesh,
        in_specs=(P("db", None, "query", None), P(None, "db"), P("db", None), P(), P()),
        out_specs=P("db", None, "query", None),
        check_vma=False,
    )
```

profile of v0, /device:TPU:17, one launch (start us, length us, event | category | flops | bytes accessed | tf_op | source)
XLA Modules:
  0.0 335.3 jit_solution(15268145274604213155)
XLA Ops:
  7.2 6.3 %collective-permute-start = (bf16[1,3,8,128]{3,2,1,0:T(8,128)(2,1)S(1)}, bf16[1,3,8,128]{3,2,1,0:T(8,128)(2,1)S(1)}, u32[]{:S(2)}, u32[]{:S(2)}) collective-permute-start(bf16[1,3,8,128]{3,2,1,0:T(8,128)(2,1)S(1)} %convert_element_type.45), channel_id=1, source_target_pairs={{0,240},{16,0},{32,16},{48,32},{64,48},{80,64},{96,80},{112,96},{1... | collective-permute-start | bytes 18440 | tf_op jit(solution)/shard_map/ppermute | solution.py:11
  18.6 4.7 %multiply_reduce_fusion.2 = (f32[2048]{0:T(1024)S(1)}, f32[2048]{0:T(1024)S(1)}, f32[2048]{0:T(1024)S(1)}, f32[2048]{0:T(1024)S(1)}) fusion(bf16[432,16384]{1,0:T(8,128)(2,1)} %param.14, s32[]{:T(128)S(6)} %select_n.33, s32[]{:T(128)S(6)} %select_n.32, s32[]{:T(128)S(6)} %select_n.34, s32[]{:T(128)S(6)} %select_n.35), kind=kLoop, calls=%fused_computation.33 | loop fusion | flops 10608640 | bytes 7110672 | tf_op jit(solution)/shard_map/reduce_sum | solution.py:66
  44.0 23.5 %all_gather.17 = bf16[432,1024]{0,1:T(8,128)(2,1)S(1)} all-gather(bf16[432,64]{0,1:T(8,128)(2,1)S(1)} %copy.4668), channel_id=1, replica_groups=mesh['query'=16,'db'=16] {'db'}, dimensions={1}, use_global_device_ids=true | all-gather | bytes 940032 | tf_op jit(solution)/shard_map/all_gather | solution.py:55
  67.4 3.8 %fusion.24 = f32[1024,2048]{1,0:T(8,128)S(1)} fusion(bf16[432,1024]{0,1:T(8,128)(2,1)S(1)} %all_gather.17, bf16[432,16384]{1,0:T(8,128)(2,1)} %param.14, s32[]{:T(128)S(6)} %select_n.35), kind=kOutput, calls=%fused_computation.37 | convolution fusion | flops 1811939328 | bytes 11042820 | tf_op jit(solution)/shard_map/dot_general | solution.py:67
  71.3 8.5 %fusion.27 = f32[1024,2048]{1,0:T(8,128)} fusion(bf16[432,1024]{0,1:T(8,128)(2,1)S(1)} %all_gather.17, bf16[432,16384]{1,0:T(8,128)(2,1)} %param.14, s32[]{:T(128)S(6)} %select_n.34), kind=kOutput, calls=%fused_computation.40 | convolution fusion | flops 1811939328 | bytes 11042820 | tf_op jit(solution)/shard_map/dot_general | solution.py:67
  79.8 6.5 %fusion.9 = (f32[1024]{0:T(1024)S(1)}, f32[1024,2048]{1,0:T(8,128)}) fusion(f32[2048]{0:T(1024)S(1)} %get-tuple-element.217, f32[1024]{0:T(1024)S(1)} %get-tuple-element.266, f32[1024]{0:T(1024)S(1)} %get-tuple-element.265, bf16[432,1024]{0,1:T(8,128)(2,1)S(1)} %all_gather.17, bf16[432,16384]{1,0:T(8,128)(2,1)} %param.14, s32[]{:T(128)S(6)} %select_n.32), kind=kOutput, calls=%fused_computation.23 | convolution fusion | flops 1820326912 | bytes 11063300 | tf_op jit(solution)/shard_map/dot_general | solution.py:67
  86.3 12.9 %fusion.2 = (f32[1024]{0:T(1024)S(1)}, f32[1024]{0:T(1024)S(1)}, f32[1024]{0:T(1024)S(1)}, f32[1024]{0:T(1024)S(1)}, f32[1024,2048]{1,0:T(8,128)}) fusion(f32[1024,2048]{1,0:T(8,128)} %get-tuple-element.272, f32[1024]{0:T(1024)S(1)} %get-tuple-element.271, f32[2048]{0:T(1024)S(1)} %get-tuple-element.217, f32[1024]{0:T(1024)S(1)} %get-tuple-element.266, ...), kind=kOutput, calls=%fused_computation.16 | convolution fusion | flops 1847586816 | bytes 36270084 | tf_op jit(solution)/shard_map/dot_general | solution.py:67
  99.2 5.8 %fusion.15 = f32[432,1024]{1,0:T(8,128)S(1)} fusion(f32[1024,2048]{1,0:T(8,128)} %fusion.27, f32[1024]{0:T(1024)S(1)} %get-tuple-element.248, f32[2048]{0:T(1024)S(1)} %get-tuple-element.218, f32[1024]{0:T(1024)S(1)} %get-tuple-element.266, f32[1024]{0:T(1024)S(1)} %get-tuple-element.265, bf16[432,16384]{1,0:T(8,128)(2,1)} %param.14, s32[]{:T(128)S(6)} %select_n.34), kind=kOutput, calls=%fused_computation.28 | convolution fusion | flops 1822425088 | bytes 11948036 | tf_op jit(solution)/shard_map/dot_general | solution.py:75
  105.1 4.3 %fusion.13 = f32[432,1024]{1,0:T(8,128)S(1)} fusion(f32[1024,2048]{1,0:T(8,128)S(1)} %fusion.24, f32[1024]{0:T(1024)S(1)} %get-tuple-element.250, f32[2048]{0:T(1024)S(1)} %get-tuple-element.219, f32[1024]{0:T(1024)S(1)} %get-tuple-element.266, f32[1024]{0:T(1024)S(1)} %get-tuple-element.265, bf16[432,16384]{1,0:T(8,128)(2,1)} %param.14, s32[]{:T(128)S(6)} %select_n.35), kind=kOutput, calls=%fused_computation.27 | convolution fusion | flops 1822425088 | bytes 11948036 | tf_op jit(solution)/shard_map/dot_general | solution.py:75
  109.5 4.3 %fusion.17 = f32[432,1024]{1,0:T(8,128)S(1)} fusion(f32[1024,2048]{1,0:T(8,128)S(1)} %bitcast.375, f32[1024]{0:T(1024)S(1)} %get-tuple-element.246, f32[2048]{0:T(1024)S(1)} %get-tuple-element.216, f32[1024]{0:T(1024)S(1)} %get-tuple-element.266, f32[1024]{0:T(1024)S(1)} %get-tuple-element.265, bf16[432,16384]{1,0:T(8,128)(2,1)} %param.14, s32[]{:T(128)S(6)} %select_n.33), kind=kOutput, calls=%fused_computation.29 | convolution fusion | flops 1822425088 | bytes 11948036 | tf_op jit(solution)/shard_map/dot_general | solution.py:75
  113.9 6.3 %multiply_add_fusion.1 = f32[432,1024]{1,0:T(8,128)} fusion(f32[432,1024]{1,0:T(8,128)S(1)} %fusion.13, f32[432,1024]{1,0:T(8,128)S(1)} %fusion.15, f32[432,1024]{1,0:T(8,128)S(1)} %fusion.17, f32[1024,2048]{1,0:T(8,128)S(1)} %bitcast.393, f32[1024]{0:T(1024)S(1)} %get-tuple-element.271, f32[2048]{0:T(1024)S(1)} %get-tuple-element.217, ...), kind=kOutput, calls=%fused_computation.35 | convolution fusion | flops 1825521664 | bytes 17272836 | tf_op jit(solution)/shard_map/dot_general | solution.py:75
  120.2 11.0 %fusion.4 = (f32[1024]{0:T(1024)S(1)}, f32[1024]{0:T(1024)S(1)}, f32[1024]{0:T(1024)S(1)}) fusion(f32[1024,2048]{1,0:T(8,128)} %get-tuple-element.273, f32[1024]{0:T(1024)S(1)} %get-tuple-element.246, f32[2048]{0:T(1024)S(1)} %get-tuple-element.216, f32[1024]{0:T(1024)S(1)} %get-tuple-element.266, f32[1024]{0:T(1024)S(1)} %get-tuple-element.265, ...), kind=kLoop, calls=%fused_computation.18 | loop fusion | flops 31454208 | bytes 25223168 | tf_op jit(solution)/shard_map/reduce_sum | solution.py:74
  131.3 25.9 %all-gather.2 = f32[16,1,1024]{2,1,0:T(1,128)S(1)} all-gather(f32[1,1,1024]{2,1,0:T(1,128)S(1)} %get-tuple-element.262), channel_id=1, replica_groups=mesh['query'=16,'db'=16] {'db'}, dimensions={0}, use_global_device_ids=true | all-gather | bytes 69632 | tf_op jit(solution)/shard_map/all_gather | solution.py:15
  157.2 19.5 %all-gather.1 = f32[16,1,1024]{2,1,0:T(1,128)S(1)} all-gather(f32[1,1,1024]{2,1,0:T(1,128)S(1)} %get-tuple-element.263), channel_id=1, replica_groups=mesh['query'=16,'db'=16] {'db'}, dimensions={0}, use_global_device_ids=true | all-gather | bytes 69632 | tf_op jit(solution)/shard_map/all_gather | solution.py:15
  176.8 106.6 %all-gather.5.cloned.1.call-done = f32[6912,1024]{1,0:T(8,128)} async-done(((f32[432,1024]{1,0:T(8,128)}), f32[6912,1024]{1,0:T(8,128)}) %all-gather.5.cloned.1.call-update) | async-done | bytes 28311568 | tf_op jit(solution)/shard_map/all_gather | solution.py:15
  285.0 34.9 %while.22 = (s32[]{:T(128)}, f32[1024]{0:T(1024)S(1)}, f32[1024]{0:T(1024)S(1)}, f32[432,1024]{1,0:T(8,128)S(1)}, f32[16,1024]{1,0:T(8,128)S(1)}, /*index=5*/f32...) while((s32[]{:T(128)}, f32[1024]{0:T(1024)S(1)}, f32[1024]{0:T(1024)S(1)}, ...), condition=%wide.region_13.0_spmd, body=%wide.region_12.0_spmd.sunk | while | flops 1333253 | bytes 5365903 | solution.py:21
  285.1 2.3 fusion.50
  287.4 2.3 fusion.50
  289.7 2.3 fusion.50
  292.1 2.3 fusion.50
  294.4 2.3 fusion.50
  296.7 2.3 fusion.50
  299.1 2.3 fusion.50
  301.4 2.3 fusion.50
  (382 shorter events, 47.0 us)
Async XLA Ops:
  6.5 276.9 %all-gather.5.cloned.1.call-start = ((), (), s32[]{:S(2)}) async-start(), calls=%async_computation | async-start | bytes 30081024 | tf_op jit(solution)/shard_map/all_gather | solution.py:15
  7.2 16.0 %collective-permute-start = (bf16[1,3,8,128]{3,2,1,0:T(8,128)(2,1)S(1)}, bf16[1,3,8,128]{3,2,1,0:T(8,128)(2,1)S(1)}, u32[]{:S(2)}, u32[]{:S(2)}) collective-permute-start(bf16[1,3,8,128]{3,2,1,0:T(8,128)(2,1)S(1)} %convert_element_type.45), channel_id=1, source_target_pairs={{0,240},{16,0},{32,16},{48,32},{64,48},{80,64},{96,80},{112,96},{1... | collective-permute-start | bytes 18440 | tf_op jit(solution)/shard_map/ppermute | solution.py:11
  71.3 33.9 %copy-start = (f32[1024,2048]{1,0:T(8,128)}, f32[1024,2048]{1,0:T(8,128)S(1)}, u32[]{:S(2)}) copy-start(f32[1024,2048]{1,0:T(8,128)S(1)} %fusion.24) | copy-start | bytes 25165828
  99.2 10.2 %slice-start = ((s8[8388608]{0:T(1024)(128)(4,1)}), s8[4194304]{0:T(1024)(128)(4,1)S(1)}, s32[]{:S(2)}) async-start(s8[8388608]{0:T(1024)(128)(4,1)} %bitcast.374), calls=%async_computation.1 | async-start | bytes 8388608
  105.1 4.4 %slice-start.1 = ((s8[8388608]{0:T(1024)(128)(4,1)}), s8[4194304]{0:T(1024)(128)(4,1)S(1)}, s32[]{:S(2)}) async-start(s8[8388608]{0:T(1024)(128)(4,1)} %bitcast.374), calls=%async_computation.2 | async-start | bytes 8388608
  105.1 8.7 %slice-start.2 = ((s8[8388608]{0:T(1024)(128)(4,1)}), s8[4194304]{0:T(1024)(128)(4,1)S(1)}, s32[]{:S(2)}) async-start(s8[8388608]{0:T(1024)(128)(4,1)} %bitcast.392), calls=%async_computation.3 | async-start | bytes 8388608
  109.5 4.3 %slice-start.3 = ((s8[8388608]{0:T(1024)(128)(4,1)}), s8[4194304]{0:T(1024)(128)(4,1)S(1)}, s32[]{:S(2)}) async-start(s8[8388608]{0:T(1024)(128)(4,1)} %bitcast.392), calls=%async_computation.4 | async-start | bytes 8388608
  285.0 38.8 %copy-start.2 = (f32[16]{0:T(128)S(1)}, f32[16]{0:T(128)}, u32[]{:S(2)}) copy-start(f32[16]{0:T(128)} %param.16) | copy-start | bytes 196
  285.0 40.8 %copy-start.3 = (f32[16]{0:T(128)S(1)}, f32[16]{0:T(128)}, u32[]{:S(2)}) copy-start(f32[16]{0:T(128)} %param.17) | copy-start | bytes 196
  285.0 42.8 %copy-start.1 = (f32[1,3,8,128]{3,2,1,0:T(8,128)S(1)}, f32[1,3,8,128]{3,2,1,0:T(8,128)}, u32[]{:S(2)}) copy-start(f32[1,3,8,128]{3,2,1,0:T(8,128)} %param.13) | copy-start | bytes 36868
  321.9 5.8 %collective-permute-start.1 = (f32[1,3,8,128]{3,2,1,0:T(8,128)S(1)}, f32[1,3,8,128]{3,2,1,0:T(8,128)S(1)}, u32[]{:S(2)}, u32[]{:S(2)}) collective-permute-start(f32[1,3,8,128]{3,2,1,0:T(8,128)S(1)} %slice.736), channel_id=1, source_target_pairs={{0,16},{16,32},{32,48},{48,64},{64,80},{80,96},{96,112},{112,128},... | collective-permute-start | bytes 36872 | tf_op jit(solution)/shard_map/ppermute | solution.py:11
Sparse Core Ops, SparseCore 0:
  120.3 163.0 all-gather.4
where the time goes:
time: 338 us; the launch traced here: 335 us
  waiting for transfers between devices  107 us (32%)
  blocking collectives  68.9 us (20%)
  matrix products  52.5 us (16%)
  other arithmetic  51.8 us (15%)
  local copies, waits for them, and re-layouts  27.1 us (8%)
  between operations  19.5 us (6%)
  starting transfers between devices  8.19 us (2%)
    all_gather x1, waiting for transfers between devices, combined_all(): everything = jax.tree.map(lambda part: lax.all_gather(part, axis), value)  107 us
    all_gather x2, blocking collectives, combined_all(): everything = jax.tree.map(lambda part: lax.all_gather(part, axis), value)  45.4 us
    add x15, other arithmetic, combine(): numerator = first[2] * factor_one[None, :] + second[2] * factor_two[None, :]  34 us
    dot_general x4, matrix products, on_device(): lax.dot_general(gathered, window, (((0,), (0,)), ((), ())), preferred_ele...  31.8 us
    all_gather x1, blocking collectives, on_device(): gathered = lax.all_gather(extract(extended), 'db', axis=1, tiled=True)  23.5 us
    dot_general x4, matrix products, on_device(): lax.dot_general(window, raw.astype(jnp.bfloat16), (((1,), (1,)), ((), ())...  20.8 us
    slice x144, local copies, waits for them, and re-layouts, extract(): pixels[:, :, row_shift:row_shift + height:4, col_shift:col_shift + across:4]  18.4 us
    reduce_sum x1, other arithmetic, on_device(): totals = totals * rescale + jnp.sum(raw, axis=1)  11 us
  transfers between devices with their start and end apart: 3, of which 1 were waited for; matrix products, arithmetic and copies ran while one was open for 6% of the time, Pallas kernels for 0%

commit v1 on v0

v1 whole, which is shorter than its diff:
```python
import functools

import jax
import jax.numpy as jnp
from jax import lax
from jax.experimental import pallas as pl
from jax.experimental.pallas import tpu as pltpu
from jax.sharding import PartitionSpec as P

MESH = pl.DeviceIdType.MESH
F32 = jnp.float32
BF16 = jnp.bfloat16
BLOCK = 2048
PREP = 512
STEP = 512
LOG2E = 1.4426950408889634


def step_kernel(nq, nd, noisy_ref, db_hbm, picked_ref, now_ref, next_ref, out_ref,
                dbv, kt, sbuf0, sbuf1, qbuf, acc, sel, perm, ystack, zbuf, gath, stat, pstage, precv,
                dbsem, gss, grs, sts, srs, pss, prs):
    ng = nd // 4
    keys = kt.shape[0]
    q = lax.axis_index("query")
    d = lax.axis_index("db")
    up = lax.rem(q + nq - 1, nq)
    down = lax.rem(q + 1, nq)
    lo_me = d // ng
    g_me = lax.rem(d, ng)

    def db_copy(i):
        return pltpu.make_async_copy(db_hbm.at[:, pl.ds(i * BLOCK, BLOCK)], dbv.at[i], dbsem.at[i])

    for i in range(dbv.shape[0]):
        db_copy(i).start()

    barrier = pltpu.get_barrier_semaphore()

    def greet(row, first):
        def body(o, carry):
            pl.semaphore_signal(barrier, inc=1, device_id=(row, lax.rem(d + o, nd)), device_id_type=MESH)
            return carry
        lax.fori_loop(first, nd, body, 0)

    greet(q, 1)
    greet(up, 0)
    greet(down, 0)

    own_tile = noisy_ref[0].astype(BF16)
    gath[0, lo_me, g_me] = own_tile

    def fill_sel(j, carry):
        lane = lax.broadcasted_iota(jnp.int32, (512, 128), 1)
        row = lax.broadcasted_iota(jnp.int32, (512, 128), 0)
        want = (lane // 32) * 128 + (4 * (lane % 32) + j) % 128
        sel[:, pl.ds(pl.multiple_of(j * 128, 128), 128)] = jnp.where(row == want, 1.0, 0.0).astype(BF16)
        return carry

    lax.fori_loop(0, 12, fill_sel, 0)

    def fill_perm(r, carry):
        row = lax.broadcasted_iota(jnp.int32, (144, 192), 0)
        col = lax.broadcasted_iota(jnp.int32, (144, 192), 1)
        want = (row % 12) * 16 + 4 * r + row // 12
        perm[pl.ds(pl.multiple_of(r * 144, 144), 144), :] = jnp.where(col == want, 1.0, 0.0).astype(BF16)
        return carry

    lax.fori_loop(0, 2, fill_perm, 0)

    pl.semaphore_wait(barrier, 3 * nd - 1)

    def tile_same(src):
        lo, g = src // ng, lax.rem(src, ng)
        return gath.at[0, lo, g]

    def send_same(o, carry):
        pltpu.make_async_remote_copy(
            src_ref=gath.at[0, lo_me, g_me], dst_ref=gath.at[0, lo_me, g_me],
            send_sem=gss.at[o], recv_sem=grs.at[d],
            device_id=(q, lax.rem(d + o, nd)), device_id_type=MESH).start()
        return carry

    def send_up(o, carry):
        pltpu.make_async_remote_copy(
            src_ref=gath.at[0, lo_me, g_me], dst_ref=gath.at[1, lo_me, g_me],
            send_sem=gss.at[nd + o], recv_sem=grs.at[nd + d],
            device_id=(up, lax.rem(d + o, nd)), device_id_type=MESH).start()
        return carry

    lax.fori_loop(1, nd, send_same, 0)
    lax.fori_loop(0, nd, send_up, 0)

    for i in range(dbv.shape[0]):
        db_copy(i).wait()

    def key_columns(i, size):
        slot = i // (BLOCK // size)
        inside = pl.multiple_of(lax.rem(i, BLOCK // size) * size, size)
        return dbv[picked_ref[0, slot], :, pl.ds(inside, size)]

    def prepare(i, carry):
        cols = key_columns(i, PREP)
        wide = cols.astype(F32)
        squares = jnp.sum(wide * wide, axis=0, keepdims=True)
        high = squares.astype(BF16).astype(F32)
        rest = squares - high
        mid = rest.astype(BF16).astype(F32)
        low = rest - mid
        row = lax.broadcasted_iota(jnp.int32, (80, PREP), 0)
        extra = jnp.where((row == 0) | (row == 3) | (row == 5), high,
                          jnp.where((row == 1) | (row == 4), mid, jnp.where(row == 2, low, 0.0)))
        full = jnp.concatenate([cols, extra.astype(BF16)], axis=0)
        kt[pl.ds(pl.multiple_of(i * PREP, PREP), PREP), :] = full.T
        return carry

    lax.fori_loop(0, keys // PREP, prepare, 0)

    def per_lane(ref, g, rows):
        lane = lax.broadcasted_iota(jnp.int32, (rows, 256), 1)
        image = (lane // 32) % 4
        value = jnp.full((rows, 256), ref[g], F32)
        for lo in range(1, 4):
            value = jnp.where(image == lo, ref[lo * ng + g], value)
        return value

    for g in range(ng):
        a = per_lane(now_ref, g, 80)
        c = -0.5 * jnp.sqrt(a)
        high = c.astype(BF16).astype(F32)
        rest = c - high
        mid = rest.astype(BF16).astype(F32)
        low = rest - mid
        row = lax.broadcasted_iota(jnp.int32, (80, 256), 0)
        extra = jnp.where(row < 3, high, jnp.where(row < 5, mid, jnp.where(row == 5, low, 0.0)))
        qbuf[g, pl.ds(432, 80), :] = extra.astype(BF16)

    def got_same(o, carry):
        src = lax.rem(d + o, nd)
        lo, g = src // ng, lax.rem(src, ng)
        pltpu.make_async_remote_copy(
            src_ref=gath.at[0, lo, g], dst_ref=gath.at[0, lo, g], send_sem=gss.at[o], recv_sem=grs.at[src],
            device_id=(q, src), device_id_type=MESH).wait_recv()
        return carry

    def got_below(o, carry):
        src = lax.rem(d + o, nd)
        lo, g = src // ng, lax.rem(src, ng)
        pltpu.make_async_remote_copy(
            src_ref=gath.at[1, lo, g], dst_ref=gath.at[1, lo, g], send_sem=gss.at[nd + o], recv_sem=grs.at[nd + src],
            device_id=(down, src), device_id_type=MESH).wait_recv()
        return carry

    lax.fori_loop(1, nd, got_same, 0)
    lax.fori_loop(0, nd, got_below, 0)

    lanes = []
    for lo in range(4):
        both = jnp.concatenate([gath[0, lo].astype(F32), gath[1, lo].astype(F32)], axis=2)
        lanes.append(both.reshape(ng * 48, 128))
    rows = jnp.concatenate(lanes, axis=1).astype(BF16)
    for j in range(12):
        y = jnp.dot(rows, sel[:, j * 128:(j + 1) * 128], preferred_element_type=F32).astype(BF16)
        for g in range(ng):
            for c in range(3):
                ystack[c, j * 16:(j + 1) * 16, g * 128:(g + 1) * 128] = y[(g * 3 + c) * 16:(g * 3 + c + 1) * 16, :]
    for c in range(3):
        placed = jnp.dot(perm[...], ystack[c], preferred_element_type=F32).astype(BF16)
        for g in range(ng):
            for r in range(2):
                qbuf[g, c * 144:(c + 1) * 144, r * 128:(r + 1) * 128] = (
                    placed[r * 144:(r + 1) * 144, g * 128:(g + 1) * 128])

    sbufs = (sbuf0, sbuf1)
    steps = keys // STEP

    def logits(g, i):
        part = pl.ds(pl.multiple_of(i * STEP, STEP), STEP)
        s = jnp.dot(kt[part, :], qbuf[g], preferred_element_type=F32)
        sbufs[g % 2][part, :] = s
        return jnp.max(s.reshape(STEP // 8, 8, 256), axis=0)

    def weigh(g, i, top, scale):
        part = pl.ds(pl.multiple_of(i * STEP, STEP), STEP)
        p = jnp.exp2((sbufs[g % 2][part, :] - top) * scale)
        cols = key_columns(i, STEP)
        acc[g] += jnp.dot(cols, p.astype(BF16), preferred_element_type=F32)
        return jnp.sum(p.reshape(STEP // 8, 8, 256), axis=0)

    def scale_of(g):
        a = per_lane(now_ref, g, 1)
        return LOG2E * jnp.sqrt(a) / (1.0 - a)

    def stat_send(g, o):
        return pltpu.make_async_remote_copy(
            src_ref=stat.at[g, d], dst_ref=stat.at[g, d], send_sem=sts.at[g, o], recv_sem=srs.at[g, d],
            device_id=(q, lax.rem(d + o, nd)), device_id_type=MESH)

    def share(g, top, total):
        whole = jnp.concatenate([top[:, :128], top[:, 128:], total[:, :128], total[:, 128:],
                                 jnp.zeros((4, 128), F32)], axis=0)
        stat[g, d] = whole

        def body(o, carry):
            stat_send(g, o).start()
            return carry

        lax.fori_loop(1, nd, body, 0)

    def pixel_send(g, lo, half):
        dest = lo * ng + g
        return pltpu.make_async_remote_copy(
            src_ref=pstage.at[g, lo, half], dst_ref=precv.at[half, d],
            send_sem=pss.at[g, 2 * lo + half], recv_sem=prs.at[half, d],
            device_id=(down if half else q, dest), device_id_type=MESH)

    def finish(g, top, scale):
        def body(o, carry):
            src = lax.rem(d + o, nd)
            pltpu.make_async_remote_copy(
                src_ref=stat.at[g, src], dst_ref=stat.at[g, src], send_sem=sts.at[g, o], recv_sem=srs.at[g, src],
                device_id=(q, src), device_id_type=MESH).wait_recv()
            return carry

        lax.fori_loop(1, nd, body, 0)
        every = stat[g]
        tops = jnp.concatenate([every[:, 0], every[:, 1]], axis=1)
        totals = jnp.concatenate([every[:, 2], every[:, 3]], axis=1)
        highest = jnp.max(tops, axis=0, keepdims=True)
        total = jnp.sum(totals * jnp.exp2((tops - highest) * scale), axis=0, keepdims=True)
        factor = jnp.exp2((top - highest) * scale) / (9.0 * total)
        num = acc[g] * factor
        for c in range(3):
            first = num[c * 144:(c + 1) * 144, :128]
            second = num[c * 144:(c + 1) * 144, 128:]
            zbuf[c * 192:c * 192 + 48, :] = first[:48]
            zbuf[c * 192 + 48:c * 192 + 144, :] = first[48:] + second[:96]
            zbuf[c * 192 + 144:c * 192 + 192, :] = second[96:]
        parts = []
        for j in range(12):
            parts.append(zbuf[pl.ds(j, 48, stride=12), :])
        flat = jnp.concatenate(parts, axis=1)
        high = flat.astype(BF16)
        low = (flat - high.astype(F32)).astype(BF16)
        both = jnp.concatenate([high, low], axis=0)
        pix = lax.dot_general(both, sel[...], (((1,), (1,)), ((), ())), preferred_element_type=F32)
        pix = pix[:48] + pix[48:]
        for lo in range(4):
            tile = pix[:, lo * 128:(lo + 1) * 128].reshape(3, 16, 128)
            pstage[g, lo, 0] = tile[:, :8]
            pstage[g, lo, 1] = tile[:, 8:]
        for lo in range(4):
            @pl.when(lo * ng + g != d)
            def _():
                pixel_send(g, lo, 0).start()
            pixel_send(g, lo, 1).start()

    neg = jnp.full((8, 256), -jnp.inf, F32)
    tops = {}
    scales = {}
    for t in range(ng + 1):
        if t >= 1:
            scales[t - 1] = scale_of(t - 1)
            acc[t - 1] = jnp.zeros((432, 256), F32)

        def body(i, carry, t=t):
            best, total = carry
            if t < ng:
                best = jnp.maximum(best, logits(t, i))
            if t >= 1:
                total = total + weigh(t - 1, i, tops[t - 1], scales[t - 1])
            return best, total

        best, total = lax.fori_loop(0, steps, body, (neg, jnp.zeros((8, 256), F32)))
        if t < ng:
            tops[t] = jnp.max(best, axis=0, keepdims=True)
        if t >= 1:
            share(t - 1, tops[t - 1], jnp.sum(total, axis=0, keepdims=True))
        if t >= 2:
            finish(t - 2, tops[t - 2], scales[t - 2])
    finish(ng - 1, tops[ng - 1], scales[ng - 1])

    def got_own(o, carry):
        src = lax.rem(d + o, nd)
        pltpu.make_async_remote_copy(
            src_ref=precv.at[0, src], dst_ref=precv.at[0, src], send_sem=pss.at[0, 0], recv_sem=prs.at[0, src],
            device_id=(q, src), device_id_type=MESH).wait_recv()
        return carry

    def got_spill(o, carry):
        src = lax.rem(d + o, nd)
        pltpu.make_async_remote_copy(
            src_ref=precv.at[1, src], dst_ref=precv.at[1, src], send_sem=pss.at[0, 1], recv_sem=prs.at[1, src],
            device_id=(up, src), device_id_type=MESH).wait_recv()
        return carry

    lax.fori_loop(1, nd, got_own, 0)
    lax.fori_loop(0, nd, got_spill, 0)
    precv[0, d] = pstage[g_me, lo_me, 0]
    denoised = jnp.sum(precv[0], axis=0) + jnp.sum(precv[1], axis=0)
    signal = jnp.full((1, 8, 128), now_ref[d], F32)
    after = jnp.full((1, 8, 128), next_ref[d], F32)
    noise = (noisy_ref[0] - jnp.sqrt(signal) * denoised) / jnp.sqrt(1.0 - signal)
    out_ref[0] = jnp.sqrt(after) * denoised + jnp.sqrt(1.0 - after) * noise

    def sent_same(o, carry):
        pltpu.make_async_remote_copy(
            src_ref=gath.at[0, lo_me, g_me], dst_ref=gath.at[0, lo_me, g_me],
            send_sem=gss.at[o], recv_sem=grs.at[d],
            device_id=(q, lax.rem(d + o, nd)), device_id_type=MESH).wait_send()
        return carry

    def sent_up(o, carry):
        pltpu.make_async_remote_copy(
            src_ref=gath.at[0, lo_me, g_me], dst_ref=gath.at[1, lo_me, g_me],
            send_sem=gss.at[nd + o], recv_sem=grs.at[nd + d],
            device_id=(up, lax.rem(d + o, nd)), device_id_type=MESH).wait_send()
        return carry

    lax.fori_loop(1, nd, sent_same, 0)
    lax.fori_loop(0, nd, sent_up, 0)
    for g in range(ng):
        def sent_stat(o, carry, g=g):
            stat_send(g, o).wait_send()
            return carry

        lax.fori_loop(1, nd, sent_stat, 0)
        for lo in range(4):
            @pl.when(lo * ng + g != d)
            def _():
                pixel_send(g, lo, 0).wait_send()
            pixel_send(g, lo, 1).wait_send()


def on_device(nq, nd, noisy, database, picked, now, after):
    ng = nd // 4
    windows = picked.shape[1]
    keys = windows * BLOCK
    vmem = pl.BlockSpec(memory_space=pltpu.VMEM)
    smem = pl.BlockSpec(memory_space=pltpu.SMEM)
    dma = pltpu.SemaphoreType.DMA
    return pl.pallas_call(
        functools.partial(step_kernel, nq, nd),
        out_shape=jax.ShapeDtypeStruct(noisy.shape, F32),
        in_specs=[vmem, pl.BlockSpec(memory_space=pl.ANY), smem, smem, smem],
        out_specs=vmem,
        scratch_shapes=[
            pltpu.VMEM((database.shape[1] // BLOCK, database.shape[0], BLOCK), BF16),
            pltpu.VMEM((keys, 512), BF16),
            pltpu.VMEM((keys, 256), F32),
            pltpu.VMEM((keys, 256), F32),
            pltpu.VMEM((ng, 512, 256), BF16),
            pltpu.VMEM((ng, 432, 256), F32),
            pltpu.VMEM((512, 1536), BF16),
            pltpu.VMEM((288, 192), BF16),
            pltpu.VMEM((3, 192, ng * 128), BF16),
            pltpu.VMEM((576, 128), F32),
            pltpu.VMEM((2, 4, ng, 3, 8, 128), BF16),
            pltpu.VMEM((ng, nd, 8, 128), F32),
            pltpu.VMEM((ng, 4, 2, 3, 8, 128), F32),
            pltpu.VMEM((2, nd, 3, 8, 128), F32),
            dma((database.shape[1] // BLOCK,)),
            dma((2 * nd,)),
            dma((2 * nd,)),
            dma((ng, nd)),
            dma((ng, nd)),
            dma((ng, 8)),
            dma((2, nd)),
        ],
        compiler_params=pltpu.CompilerParams(
            collective_id=0, has_side_effects=True, vmem_limit_bytes=64_000_000),
    )(noisy, database, picked, now, after)


def solution(mesh):
    return jax.shard_map(
        functools.partial(on_device, mesh.shape["query"], mesh.shape["db"]),
        mesh=mesh,
        in_specs=(P("db", None, "query", None), P(None, "db"), P("db", None), P(), P()),
        out_specs=P("db", None, "query", None),
        check_vma=False,
    )
```

time: 338 us -> 67.4 us (0.20)
  waiting for transfers between devices: 107 us -> 0 us
  blocking collectives: 68.9 us -> 0 us
  Pallas kernels: 0 us -> 65.9 us
  matrix products: 52.5 us -> 0 us
  other arithmetic: 51.8 us -> 0 us
  local copies, waits for them, and re-layouts: 27.1 us -> 1.31 us
  between operations: 19.5 us -> 0.01 us
  starting transfers between devices: 8.19 us -> 0 us
    all_gather x1 -> x0, waiting for transfers between devices: 107 us -> none  [combined_all(): everything = jax.tree.map(lambda part: lax.all_gather(part, axis), value)]
    all_gather x3 -> x0, blocking collectives: 68.9 us -> none  [the longest x2 45.4 us: combined_all(): everything = jax.tree.map(lambda part: lax.all_gather(part, axis), value)]
    pallas_call x0 -> x1, Pallas kernels: none -> 65.9 us  [on_device(): pl.pallas_call(functools.partial(step_kernel, nq, nd), out_shape=jax.Shap...]
    dot_general x8 -> x0, matrix products: 52.5 us -> none  [the longest x4 31.8 us: on_device(): lax.dot_general(gathered, window, (((0,), (0,)), ((), ())), preferred_ele...]
    add x33 -> x0, other arithmetic: 35.2 us -> none  [the longest x15 34 us: combine(): numerator = first[2] * factor_one[None, :] + second[2] * factor_two[None, :]]
    slice x150 -> x0, local copies, waits for them, and re-layouts: 21.4 us -> none  [the longest x144 18.4 us: extract(): pixels[:, :, row_shift:row_shift + height:4, col_shift:col_shift + across:4]]
    reduce_sum x2 -> x0, other arithmetic: 15.7 us -> none  [the longest x1 11 us: on_device(): totals = totals * rescale + jnp.sum(raw, axis=1)]
    ppermute x2 -> x0, starting transfers between devices: 8.18 us -> none  [shifted(): lax.ppermute(value, axis, [(i, (i + by) % count) for i in range(count)])]
  transfers between devices with their start and end apart: 3 -> 0, of which waited for: 1 -> 0; matrix products, arithmetic and copies ran while one was open for 6% -> 0% of each run, Pallas kernels for 0% -> 0%
where the time goes in v1:
time: 67.4 us; the launch traced here: 67.2 us
  Pallas kernels  65.9 us (98%)
  local copies, waits for them, and re-layouts  1.31 us (2%)
    pallas_call x1, Pallas kernels, on_device(): pl.pallas_call(functools.partial(step_kernel, nq, nd), out_shape=jax.Shap...  65.9 us

profile of v1, /device:TPU:17, one launch (start us, length us, event | category | flops | bytes accessed | tf_op | source)
XLA Modules:
  0.0 67.2 jit_solution(12974098428816188899)
XLA Ops:
  0.0 65.9 %shard_map.55 = f32[1,3,8,128]{3,2,1,0:T(8,128)} custom-call(f32[1,3,8,128]{3,2,1,0:T(8,128)} %noisy_ref.1, bf16[432,16384]{1,0:T(8,128)(2,1)} %db_hbm.1, s32[1,4]{1,0:T(1,128)} %picked_ref.1, f32[16]{0:T(128)} %now_ref.1, f32[16]{0:T(128)} %next_ref.1), custom_call_target="tpu_custom_call" | custom-call | tf_op jit(solution)/shard_map/pallas_call | solution.py:341
  65.9 1.3 %copy.7 = f32[1,3,8,128]{3,2,1,0:T(8,128)} copy(f32[1,3,8,128]{3,2,1,0:T(8,128)} %shard_map.55) | data formatting | bytes 24576

commit v2 on v1

--- a/solution.py
+++ b/solution.py
@@ -12,12 +12,14 @@
 BF16 = jnp.bfloat16
 BLOCK = 2048
 PREP = 512
-STEP = 512
+STEP = 2048
+SUB = 512
+CHUNK = 32
 LOG2E = 1.4426950408889634
 
 
 def step_kernel(nq, nd, noisy_ref, db_hbm, picked_ref, now_ref, next_ref, out_ref,
-                dbv, kt, sbuf0, sbuf1, qbuf, acc, sel, perm, ystack, zbuf, gath, stat, pstage, precv,
+                dbv, kt, sbuf0, sbuf1, wbuf0, wbuf1, qbuf, acc, sel, perm, ystack, zbuf, gath, stat, pstage, precv,
                 dbsem, gss, grs, sts, srs, pss, prs):
     ng = nd // 4
     keys = kt.shape[0]
@@ -42,12 +44,12 @@
             return carry
         lax.fori_loop(first, nd, body, 0)
 
+    for row in (up, down):
+        pl.semaphore_signal(barrier, inc=1, device_id=(row, d), device_id_type=MESH)
     greet(q, 1)
-    greet(up, 0)
-    greet(down, 0)
 
     own_tile = noisy_ref[0].astype(BF16)
-    gath[0, lo_me, g_me] = own_tile
+    gath[lo_me, g_me, 0] = own_tile
 
     def fill_sel(j, carry):
         lane = lax.broadcasted_iota(jnp.int32, (512, 128), 1)
@@ -67,28 +69,34 @@
 
     lax.fori_loop(0, 2, fill_perm, 0)
 
-    pl.semaphore_wait(barrier, 3 * nd - 1)
-
-    def tile_same(src):
+    pl.semaphore_wait(barrier, nd + 1)
+
+    def column_copy():
+        return pltpu.make_async_remote_copy(
+            src_ref=gath.at[lo_me, g_me, 0], dst_ref=gath.at[lo_me, g_me, 1],
+            send_sem=gss.at[0], recv_sem=grs.at[nd + d], device_id=(up, d), device_id_type=MESH)
+
+    def row_copy(half, o):
+        return pltpu.make_async_remote_copy(
+            src_ref=gath.at[lo_me, g_me, half], dst_ref=gath.at[lo_me, g_me, half],
+            send_sem=gss.at[half * nd + o], recv_sem=grs.at[half * nd + d],
+            device_id=(q, lax.rem(d + o, nd)), device_id_type=MESH)
+
+    def arrival(half, src):
         lo, g = src // ng, lax.rem(src, ng)
-        return gath.at[0, lo, g]
-
-    def send_same(o, carry):
-        pltpu.make_async_remote_copy(
-            src_ref=gath.at[0, lo_me, g_me], dst_ref=gath.at[0, lo_me, g_me],
-            send_sem=gss.at[o], recv_sem=grs.at[d],
-            device_id=(q, lax.rem(d + o, nd)), device_id_type=MESH).start()
-        return carry
-
-    def send_up(o, carry):
-        pltpu.make_async_remote_copy(
-            src_ref=gath.at[0, lo_me, g_me], dst_ref=gath.at[1, lo_me, g_me],
-            send_sem=gss.at[nd + o], recv_sem=grs.at[nd + d],
-            device_id=(up, lax.rem(d + o, nd)), device_id_type=MESH).start()
-        return carry
-
-    lax.fori_loop(1, nd, send_same, 0)
-    lax.fori_loop(0, nd, send_up, 0)
+        return pltpu.make_async_remote_copy(
+            src_ref=gath.at[lo, g, half], dst_ref=gath.at[lo, g, half],
+            send_sem=gss.at[half * nd + 1], recv_sem=grs.at[half * nd + src],
+            device_id=(q, src), device_id_type=MESH)
+
+    def over_peers(step):
+        def body(o, carry):
+            step(o)
+            return carry
+        lax.fori_loop(1, nd, body, 0)
+
+    column_copy().start()
+    over_peers(lambda o: row_copy(0, o).start())
 
     for i in range(dbv.shape[0]):
         db_copy(i).wait()
@@ -113,7 +121,11 @@
         kt[pl.ds(pl.multiple_of(i * PREP, PREP), PREP), :] = full.T
         return carry
 
-    lax.fori_loop(0, keys // PREP, prepare, 0)
+    halfway = keys // PREP // 2
+    lax.fori_loop(0, halfway, prepare, 0)
+    column_copy().wait_recv()
+    over_peers(lambda o: row_copy(1, o).start())
+    lax.fori_loop(halfway, keys // PREP, prepare, 0)
 
     def per_lane(ref, g, rows):
         lane = lax.broadcasted_iota(jnp.int32, (rows, 256), 1)
@@ -134,35 +146,22 @@
         extra = jnp.where(row < 3, high, jnp.where(row < 5, mid, jnp.where(row == 5, low, 0.0)))
         qbuf[g, pl.ds(432, 80), :] = extra.astype(BF16)
 
-    def got_same(o, carry):
-        src = lax.rem(d + o, nd)
-        lo, g = src // ng, lax.rem(src, ng)
-        pltpu.make_async_remote_copy(
-            src_ref=gath.at[0, lo, g], dst_ref=gath.at[0, lo, g], send_sem=gss.at[o], recv_sem=grs.at[src],
-            device_id=(q, src), device_id_type=MESH).wait_recv()
-        return carry
-
-    def got_below(o, carry):
-        src = lax.rem(d + o, nd)
-        lo, g = src // ng, lax.rem(src, ng)
-        pltpu.make_async_remote_copy(
-            src_ref=gath.at[1, lo, g], dst_ref=gath.at[1, lo, g], send_sem=gss.at[nd + o], recv_sem=grs.at[nd + src],
-            device_id=(down, src), device_id_type=MESH).wait_recv()
-        return carry
-
-    lax.fori_loop(1, nd, got_same, 0)
-    lax.fori_loop(0, nd, got_below, 0)
+    over_peers(lambda o: arrival(0, lax.rem(d + o, nd)).wait_recv())
+    over_peers(lambda o: arrival(1, lax.rem(d + o, nd)).wait_recv())
 
     lanes = []
     for lo in range(4):
-        both = jnp.concatenate([gath[0, lo].astype(F32), gath[1, lo].astype(F32)], axis=2)
+        both = jnp.concatenate([gath[lo, :, 0].astype(F32), gath[lo, :, 1].astype(F32)], axis=2)
         lanes.append(both.reshape(ng * 48, 128))
     rows = jnp.concatenate(lanes, axis=1).astype(BF16)
-    for j in range(12):
-        y = jnp.dot(rows, sel[:, j * 128:(j + 1) * 128], preferred_element_type=F32).astype(BF16)
+    for pair in range(6):
+        y = jnp.dot(rows, sel[:, pair * 256:(pair + 1) * 256], preferred_element_type=F32).astype(BF16)
         for g in range(ng):
             for c in range(3):
-                ystack[c, j * 16:(j + 1) * 16, g * 128:(g + 1) * 128] = y[(g * 3 + c) * 16:(g * 3 + c + 1) * 16, :]
+                for k in range(2):
+                    j = 2 * pair + k
+                    ystack[c, j * 16:(j + 1) * 16, g * 128:(g + 1) * 128] = (
+                        y[(g * 3 + c) * 16:(g * 3 + c + 1) * 16, k * 128:(k + 1) * 128])
     for c in range(3):
         placed = jnp.dot(perm[...], ystack[c], preferred_element_type=F32).astype(BF16)
         for g in range(ng):
@@ -171,20 +170,27 @@
                     placed[r * 144:(r + 1) * 144, g * 128:(g + 1) * 128])
 
     sbufs = (sbuf0, sbuf1)
+    wbufs = (wbuf0, wbuf1)
     steps = keys // STEP
 
-    def logits(g, i):
-        part = pl.ds(pl.multiple_of(i * STEP, STEP), STEP)
+    def logits(g, start):
+        part = pl.ds(start, SUB)
         s = jnp.dot(kt[part, :], qbuf[g], preferred_element_type=F32)
         sbufs[g % 2][part, :] = s
-        return jnp.max(s.reshape(STEP // 8, 8, 256), axis=0)
-
-    def weigh(g, i, top, scale):
-        part = pl.ds(pl.multiple_of(i * STEP, STEP), STEP)
-        p = jnp.exp2((sbufs[g % 2][part, :] - top) * scale)
-        cols = key_columns(i, STEP)
-        acc[g] += jnp.dot(cols, p.astype(BF16), preferred_element_type=F32)
-        return jnp.sum(p.reshape(STEP // 8, 8, 256), axis=0)
+        return jnp.max(s.reshape(SUB // 8, 8, 256), axis=0)
+
+    def weigh(g, start, top, scale):
+        total = jnp.zeros((8, 256), F32)
+        for k in range(SUB // CHUNK):
+            part = pl.ds(start + k * CHUNK, CHUNK)
+            p = jnp.exp2((sbufs[g % 2][part, :] - top) * scale)
+            wbufs[g % 2][part, :] = p.astype(BF16)
+            total = total + jnp.sum(p.reshape(CHUNK // 8, 8, 256), axis=0)
+        return total
+
+    def gather_keys(g, slot, inside, start):
+        cols = dbv[picked_ref[0, slot], :, inside:inside + SUB]
+        acc[g] += jnp.dot(cols, wbufs[g % 2][pl.ds(start, SUB), :], preferred_element_type=F32)
 
     def scale_of(g):
         a = per_lane(now_ref, g, 1)
@@ -235,14 +241,19 @@
             zbuf[c * 192:c * 192 + 48, :] = first[:48]
             zbuf[c * 192 + 48:c * 192 + 144, :] = first[48:] + second[:96]
             zbuf[c * 192 + 144:c * 192 + 192, :] = second[96:]
+        place = lax.broadcasted_iota(jnp.int32, (48, 128), 1) % 32
         parts = []
-        for j in range(12):
-            parts.append(zbuf[pl.ds(j, 48, stride=12), :])
+        for j in range(4):
+            piece = zbuf[pl.ds(j, 48, stride=12), :]
+            for k in (1, 2):
+                z = zbuf[pl.ds(4 * k + j, 48, stride=12), :]
+                piece = piece + jnp.where(place >= k, pltpu.roll(z, k, 1), pltpu.roll(z, 96 + k, 1))
+            parts.append(piece)
         flat = jnp.concatenate(parts, axis=1)
         high = flat.astype(BF16)
         low = (flat - high.astype(F32)).astype(BF16)
         both = jnp.concatenate([high, low], axis=0)
-        pix = lax.dot_general(both, sel[...], (((1,), (1,)), ((), ())), preferred_element_type=F32)
+        pix = lax.dot_general(both, sel[:, :512], (((1,), (1,)), ((), ())), preferred_element_type=F32)
         pix = pix[:48] + pix[48:]
         for lo in range(4):
             tile = pix[:, lo * 128:(lo + 1) * 128].reshape(3, 16, 128)
@@ -257,27 +268,32 @@
     neg = jnp.full((8, 256), -jnp.inf, F32)
     tops = {}
     scales = {}
-    for t in range(ng + 1):
-        if t >= 1:
+    for t in range(ng + 2):
+        if 1 <= t <= ng:
             scales[t - 1] = scale_of(t - 1)
-            acc[t - 1] = jnp.zeros((432, 256), F32)
+        if t >= 2:
+            acc[t - 2] = jnp.zeros((432, 256), F32)
 
         def body(i, carry, t=t):
             best, total = carry
-            if t < ng:
-                best = jnp.maximum(best, logits(t, i))
-            if t >= 1:
-                total = total + weigh(t - 1, i, tops[t - 1], scales[t - 1])
+            base = pl.multiple_of(i * STEP, STEP)
+            for b in range(STEP // SUB):
+                start = base + b * SUB
+                if t < ng:
+                    best = jnp.maximum(best, logits(t, start))
+                if 1 <= t <= ng:
+                    total = total + weigh(t - 1, start, tops[t - 1], scales[t - 1])
+                if t >= 2:
+                    gather_keys(t - 2, i, b * SUB, start)
             return best, total
 
         best, total = lax.fori_loop(0, steps, body, (neg, jnp.zeros((8, 256), F32)))
         if t < ng:
             tops[t] = jnp.max(best, axis=0, keepdims=True)
-        if t >= 1:
+        if 1 <= t <= ng:
             share(t - 1, tops[t - 1], jnp.sum(total, axis=0, keepdims=True))
         if t >= 2:
             finish(t - 2, tops[t - 2], scales[t - 2])
-    finish(ng - 1, tops[ng - 1], scales[ng - 1])
 
     def got_own(o, carry):
         src = lax.rem(d + o, nd)
@@ -302,22 +318,9 @@
     noise = (noisy_ref[0] - jnp.sqrt(signal) * denoised) / jnp.sqrt(1.0 - signal)
     out_ref[0] = jnp.sqrt(after) * denoised + jnp.sqrt(1.0 - after) * noise
 
-    def sent_same(o, carry):
-        pltpu.make_async_remote_copy(
-            src_ref=gath.at[0, lo_me, g_me], dst_ref=gath.at[0, lo_me, g_me],
-            send_sem=gss.at[o], recv_sem=grs.at[d],
-            device_id=(q, lax.rem(d + o, nd)), device_id_type=MESH).wait_send()
-        return carry
-
-    def sent_up(o, carry):
-        pltpu.make_async_remote_copy(
-            src_ref=gath.at[0, lo_me, g_me], dst_ref=gath.at[1, lo_me, g_me],
-            send_sem=gss.at[nd + o], recv_sem=grs.at[nd + d],
-            device_id=(up, lax.rem(d + o, nd)), device_id_type=MESH).wait_send()
-        return carry
-
-    lax.fori_loop(1, nd, sent_same, 0)
-    lax.fori_loop(0, nd, sent_up, 0)
+    column_copy().wait_send()
+    over_peers(lambda o: row_copy(0, o).wait_send())
+    over_peers(lambda o: row_copy(1, o).wait_send())
     for g in range(ng):
         def sent_stat(o, carry, g=g):
             stat_send(g, o).wait_send()
@@ -348,13 +351,15 @@
             pltpu.VMEM((keys, 512), BF16),
             pltpu.VMEM((keys, 256), F32),
             pltpu.VMEM((keys, 256), F32),
+            pltpu.VMEM((keys, 256), BF16),
+            pltpu.VMEM((keys, 256), BF16),
             pltpu.VMEM((ng, 512, 256), BF16),
             pltpu.VMEM((ng, 432, 256), F32),
             pltpu.VMEM((512, 1536), BF16),
             pltpu.VMEM((288, 192), BF16),
             pltpu.VMEM((3, 192, ng * 128), BF16),
             pltpu.VMEM((576, 128), F32),
-            pltpu.VMEM((2, 4, ng, 3, 8, 128), BF16),
+            pltpu.VMEM((4, ng, 2, 3, 8, 128), BF16),
             pltpu.VMEM((ng, nd, 8, 128), F32),
             pltpu.VMEM((ng, 4, 2, 3, 8, 128), F32),
             pltpu.VMEM((2, nd, 3, 8, 128), F32),

time: 67.4 us -> 57.3 us (0.85)
  Pallas kernels: 65.9 us -> 55.8 us
    pallas_call x1, Pallas kernels: 65.9 us -> 55.8 us  [on_device(): pl.pallas_call(functools.partial(step_kernel, nq, nd), out_shape=jax.Shap...]
where the time goes in v2:
time: 57.3 us; the launch traced here: 57.1 us
  Pallas kernels  55.8 us (97%)
  local copies, waits for them, and re-layouts  1.31 us (2%)
    pallas_call x1, Pallas kernels, on_device(): pl.pallas_call(functools.partial(step_kernel, nq, nd), out_shape=jax.Shap...  55.8 us
    unnamed x1, local copies, waits for them, and re-layouts  1.31 us

profile of v2, /device:TPU:17, one launch (start us, length us, event | category | flops | bytes accessed | tf_op | source)
XLA Modules:
  0.0 57.1 jit_solution(7634999958824022556)
XLA Ops:
  0.0 55.8 %shard_map.55 = f32[1,3,8,128]{3,2,1,0:T(8,128)} custom-call(f32[1,3,8,128]{3,2,1,0:T(8,128)} %noisy_ref.1, bf16[432,16384]{1,0:T(8,128)(2,1)} %db_hbm.1, s32[1,4]{1,0:T(1,128)} %picked_ref.1, f32[16]{0:T(128)} %now_ref.1, f32[16]{0:T(128)} %next_ref.1), custom_call_target="tpu_custom_call" | custom-call | tf_op jit(solution)/shard_map/pallas_call | solution.py:344
  55.8 1.3 %copy.7 = f32[1,3,8,128]{3,2,1,0:T(8,128)} copy(f32[1,3,8,128]{3,2,1,0:T(8,128)} %shard_map.55) | data formatting | bytes 24576

commit v3 on v2

--- a/solution.py
+++ b/solution.py
@@ -19,8 +19,8 @@
 
 
 def step_kernel(nq, nd, noisy_ref, db_hbm, picked_ref, now_ref, next_ref, out_ref,
-                dbv, kt, sbuf0, sbuf1, wbuf0, wbuf1, qbuf, acc, sel, perm, ystack, zbuf, gath, stat, pstage, precv,
-                dbsem, gss, grs, sts, srs, pss, prs):
+                dbv, kt, sbuf0, sbuf1, wbuf0, wbuf1, wbuf2, qbuf, acc, sel, perm, ystack, zbuf, tally, gath, stat, pstage, precv,
+                dbsem, rowsem, gss, grs, sts, srs, pss, prs):
     ng = nd // 4
     keys = kt.shape[0]
     q = lax.axis_index("query")
@@ -39,10 +39,8 @@
     barrier = pltpu.get_barrier_semaphore()
 
     def greet(row, first):
-        def body(o, carry):
+        for o in range(first, nd):
             pl.semaphore_signal(barrier, inc=1, device_id=(row, lax.rem(d + o, nd)), device_id_type=MESH)
-            return carry
-        lax.fori_loop(first, nd, body, 0)
 
     for row in (up, down):
         pl.semaphore_signal(barrier, inc=1, device_id=(row, d), device_id_type=MESH)
@@ -70,33 +68,28 @@
     lax.fori_loop(0, 2, fill_perm, 0)
 
     pl.semaphore_wait(barrier, nd + 1)
-
-    def column_copy():
+    for row in (up, down):
+        pl.semaphore_signal(rowsem, inc=1, device_id=(row, d), device_id_type=MESH)
+
+    def tile_copy(half, o):
         return pltpu.make_async_remote_copy(
-            src_ref=gath.at[lo_me, g_me, 0], dst_ref=gath.at[lo_me, g_me, 1],
-            send_sem=gss.at[0], recv_sem=grs.at[nd + d], device_id=(up, d), device_id_type=MESH)
-
-    def row_copy(half, o):
-        return pltpu.make_async_remote_copy(
-            src_ref=gath.at[lo_me, g_me, half], dst_ref=gath.at[lo_me, g_me, half],
-            send_sem=gss.at[half * nd + o], recv_sem=grs.at[half * nd + d],
-            device_id=(q, lax.rem(d + o, nd)), device_id_type=MESH)
-
-    def arrival(half, src):
-        lo, g = src // ng, lax.rem(src, ng)
-        return pltpu.make_async_remote_copy(
-            src_ref=gath.at[lo, g, half], dst_ref=gath.at[lo, g, half],
-            send_sem=gss.at[half * nd + 1], recv_sem=grs.at[half * nd + src],
-            device_id=(q, src), device_id_type=MESH)
-
-    def over_peers(step):
-        def body(o, carry):
+            src_ref=gath.at[lo_me, g_me, 0], dst_ref=gath.at[lo_me, g_me, half],
+            send_sem=gss.at[half], recv_sem=grs.at[half],
+            device_id=(up if half else q, lax.rem(d + o, nd)), device_id_type=MESH)
+
+    def take(region, sem):
+        pltpu.make_async_copy(region, region, sem).wait()
+
+    def tiles(half):
+        return tally.at[pl.ds(0, nd - 1 + half)]
+
+    def over_peers(step, first=1):
+        for o in range(first, nd):
             step(o)
-            return carry
-        lax.fori_loop(1, nd, body, 0)
-
-    column_copy().start()
-    over_peers(lambda o: row_copy(0, o).start())
+
+    over_peers(lambda o: tile_copy(0, o).start())
+    pl.semaphore_wait(rowsem, 2)
+    over_peers(lambda o: tile_copy(1, o).start(), 0)
 
     for i in range(dbv.shape[0]):
         db_copy(i).wait()
@@ -121,11 +114,7 @@
         kt[pl.ds(pl.multiple_of(i * PREP, PREP), PREP), :] = full.T
         return carry
 
-    halfway = keys // PREP // 2
-    lax.fori_loop(0, halfway, prepare, 0)
-    column_copy().wait_recv()
-    over_peers(lambda o: row_copy(1, o).start())
-    lax.fori_loop(halfway, keys // PREP, prepare, 0)
+    lax.fori_loop(0, keys // PREP, prepare, 0)
 
     def per_lane(ref, g, rows):
         lane = lax.broadcasted_iota(jnp.int32, (rows, 256), 1)
@@ -146,8 +135,8 @@
         extra = jnp.where(row < 3, high, jnp.where(row < 5, mid, jnp.where(row == 5, low, 0.0)))
         qbuf[g, pl.ds(432, 80), :] = extra.astype(BF16)
 
-    over_peers(lambda o: arrival(0, lax.rem(d + o, nd)).wait_recv())
-    over_peers(lambda o: arrival(1, lax.rem(d + o, nd)).wait_recv())
+    for half in range(2):
+        take(tiles(half), grs.at[half])
 
     lanes = []
     for lo in range(4):
@@ -170,27 +159,27 @@
                     placed[r * 144:(r + 1) * 144, g * 128:(g + 1) * 128])
 
     sbufs = (sbuf0, sbuf1)
-    wbufs = (wbuf0, wbuf1)
+    wbufs = (wbuf0, wbuf1, wbuf2)
     steps = keys // STEP
 
-    def logits(g, start):
-        part = pl.ds(start, SUB)
+    def logits(g, start, size):
+        part = pl.ds(start, size)
         s = jnp.dot(kt[part, :], qbuf[g], preferred_element_type=F32)
         sbufs[g % 2][part, :] = s
-        return jnp.max(s.reshape(SUB // 8, 8, 256), axis=0)
-
-    def weigh(g, start, top, scale):
+        return jnp.max(s.reshape(size // 8, 8, 256), axis=0)
+
+    def weigh(g, start, size, top, scale):
         total = jnp.zeros((8, 256), F32)
-        for k in range(SUB // CHUNK):
+        for k in range(size // CHUNK):
             part = pl.ds(start + k * CHUNK, CHUNK)
             p = jnp.exp2((sbufs[g % 2][part, :] - top) * scale)
-            wbufs[g % 2][part, :] = p.astype(BF16)
+            wbufs[g % 3][part, :] = p.astype(BF16)
             total = total + jnp.sum(p.reshape(CHUNK // 8, 8, 256), axis=0)
         return total
 
-    def gather_keys(g, slot, inside, start):
-        cols = dbv[picked_ref[0, slot], :, inside:inside + SUB]
-        acc[g] += jnp.dot(cols, wbufs[g % 2][pl.ds(start, SUB), :], preferred_element_type=F32)
+    def gather_keys(g, slot, inside, start, size):
+        cols = dbv[picked_ref[0, slot], :, inside:inside + size]
+        acc[g] += jnp.dot(cols, wbufs[g % 3][pl.ds(start, size), :], preferred_element_type=F32)
 
     def scale_of(g):
         a = per_lane(now_ref, g, 1)
@@ -198,36 +187,24 @@
 
     def stat_send(g, o):
         return pltpu.make_async_remote_copy(
-            src_ref=stat.at[g, d], dst_ref=stat.at[g, d], send_sem=sts.at[g, o], recv_sem=srs.at[g, d],
+            src_ref=stat.at[g, d], dst_ref=stat.at[g, d], send_sem=sts.at[g], recv_sem=srs.at[g],
             device_id=(q, lax.rem(d + o, nd)), device_id_type=MESH)
 
     def share(g, top, total):
         whole = jnp.concatenate([top[:, :128], top[:, 128:], total[:, :128], total[:, 128:],
                                  jnp.zeros((4, 128), F32)], axis=0)
         stat[g, d] = whole
-
-        def body(o, carry):
-            stat_send(g, o).start()
-            return carry
-
-        lax.fori_loop(1, nd, body, 0)
+        over_peers(lambda o: stat_send(g, o).start())
 
     def pixel_send(g, lo, half):
         dest = lo * ng + g
         return pltpu.make_async_remote_copy(
             src_ref=pstage.at[g, lo, half], dst_ref=precv.at[half, d],
-            send_sem=pss.at[g, 2 * lo + half], recv_sem=prs.at[half, d],
+            send_sem=pss.at[g, 2 * lo + half], recv_sem=prs.at[half],
             device_id=(down if half else q, dest), device_id_type=MESH)
 
     def finish(g, top, scale):
-        def body(o, carry):
-            src = lax.rem(d + o, nd)
-            pltpu.make_async_remote_copy(
-                src_ref=stat.at[g, src], dst_ref=stat.at[g, src], send_sem=sts.at[g, o], recv_sem=srs.at[g, src],
-                device_id=(q, src), device_id_type=MESH).wait_recv()
-            return carry
-
-        lax.fori_loop(1, nd, body, 0)
+        take(stat.at[g, pl.ds(0, nd - 1)], srs.at[g])
         every = stat[g]
         tops = jnp.concatenate([every[:, 0], every[:, 1]], axis=1)
         totals = jnp.concatenate([every[:, 2], every[:, 3]], axis=1)
@@ -268,70 +245,59 @@
     neg = jnp.full((8, 256), -jnp.inf, F32)
     tops = {}
     scales = {}
-    for t in range(ng + 2):
-        if 1 <= t <= ng:
-            scales[t - 1] = scale_of(t - 1)
-        if t >= 2:
-            acc[t - 2] = jnp.zeros((432, 256), F32)
-
-        def body(i, carry, t=t):
+    def phase(first=None, second=None, third=None):
+        size = SUB // 2 if second is not None and (first is None or third is None) else SUB
+
+        if second is not None:
+            scales[second] = scale_of(second)
+        if third is not None:
+            acc[third] = jnp.zeros((432, 256), F32)
+
+        def body(i, carry):
             best, total = carry
             base = pl.multiple_of(i * STEP, STEP)
-            for b in range(STEP // SUB):
-                start = base + b * SUB
-                if t < ng:
-                    best = jnp.maximum(best, logits(t, start))
-                if 1 <= t <= ng:
-                    total = total + weigh(t - 1, start, tops[t - 1], scales[t - 1])
-                if t >= 2:
-                    gather_keys(t - 2, i, b * SUB, start)
+            for b in range(STEP // size):
+                start = base + b * size
+                if first is not None:
+                    best = jnp.maximum(best, logits(first, start, size))
+                if second is not None:
+                    total = total + weigh(second, start, size, tops[second], scales[second])
+                if third is not None:
+                    gather_keys(third, i, b * size, start, size)
             return best, total
 
         best, total = lax.fori_loop(0, steps, body, (neg, jnp.zeros((8, 256), F32)))
-        if t < ng:
-            tops[t] = jnp.max(best, axis=0, keepdims=True)
-        if 1 <= t <= ng:
-            share(t - 1, tops[t - 1], jnp.sum(total, axis=0, keepdims=True))
-        if t >= 2:
-            finish(t - 2, tops[t - 2], scales[t - 2])
-
-    def got_own(o, carry):
-        src = lax.rem(d + o, nd)
-        pltpu.make_async_remote_copy(
-            src_ref=precv.at[0, src], dst_ref=precv.at[0, src], send_sem=pss.at[0, 0], recv_sem=prs.at[0, src],
-            device_id=(q, src), device_id_type=MESH).wait_recv()
-        return carry
-
-    def got_spill(o, carry):
-        src = lax.rem(d + o, nd)
-        pltpu.make_async_remote_copy(
-            src_ref=precv.at[1, src], dst_ref=precv.at[1, src], send_sem=pss.at[0, 1], recv_sem=prs.at[1, src],
-            device_id=(up, src), device_id_type=MESH).wait_recv()
-        return carry
-
-    lax.fori_loop(1, nd, got_own, 0)
-    lax.fori_loop(0, nd, got_spill, 0)
+        if first is not None:
+            tops[first] = jnp.max(best, axis=0, keepdims=True)
+        if second is not None:
+            share(second, tops[second], jnp.sum(total, axis=0, keepdims=True))
+        if third is not None:
+            finish(third, tops[third], scales[third])
+
+    last = ng - 1
+    for t in range(ng):
+        phase(t, t - 1 if t >= 1 else None, t - 2 if 2 <= t < last else None)
+    phase(None, last, max(last - 2, 0))
+    for t in range(max(last - 2, 0) + 1, ng):
+        phase(None, None, t)
+
+    for half in range(2):
+        take(tiles(half), gss.at[half])
+    for g in range(ng):
+        take(stat.at[g, pl.ds(0, nd - 1)], sts.at[g])
+        for lo in range(4):
+            @pl.when(lo * ng + g != d)
+            def _():
+                pixel_send(g, lo, 0).wait_send()
+            pixel_send(g, lo, 1).wait_send()
+    take(precv.at[0, pl.ds(0, nd - 1)], prs.at[0])
+    take(precv.at[1], prs.at[1])
     precv[0, d] = pstage[g_me, lo_me, 0]
     denoised = jnp.sum(precv[0], axis=0) + jnp.sum(precv[1], axis=0)
     signal = jnp.full((1, 8, 128), now_ref[d], F32)
     after = jnp.full((1, 8, 128), next_ref[d], F32)
     noise = (noisy_ref[0] - jnp.sqrt(signal) * denoised) / jnp.sqrt(1.0 - signal)
     out_ref[0] = jnp.sqrt(after) * denoised + jnp.sqrt(1.0 - after) * noise
-
-    column_copy().wait_send()
-    over_peers(lambda o: row_copy(0, o).wait_send())
-    over_peers(lambda o: row_copy(1, o).wait_send())
-    for g in range(ng):
-        def sent_stat(o, carry, g=g):
-            stat_send(g, o).wait_send()
-            return carry
-
-        lax.fori_loop(1, nd, sent_stat, 0)
-        for lo in range(4):
-            @pl.when(lo * ng + g != d)
-            def _():
-                pixel_send(g, lo, 0).wait_send()
-            pixel_send(g, lo, 1).wait_send()
 
 
 def on_device(nq, nd, noisy, database, picked, now, after):
@@ -353,23 +319,26 @@
             pltpu.VMEM((keys, 256), F32),
             pltpu.VMEM((keys, 256), BF16),
             pltpu.VMEM((keys, 256), BF16),
+            pltpu.VMEM((keys, 256), BF16),
             pltpu.VMEM((ng, 512, 256), BF16),
             pltpu.VMEM((ng, 432, 256), F32),
             pltpu.VMEM((512, 1536), BF16),
             pltpu.VMEM((288, 192), BF16),
             pltpu.VMEM((3, 192, ng * 128), BF16),
             pltpu.VMEM((576, 128), F32),
+            pltpu.VMEM((nd, 3, 8, 128), BF16),
             pltpu.VMEM((4, ng, 2, 3, 8, 128), BF16),
             pltpu.VMEM((ng, nd, 8, 128), F32),
             pltpu.VMEM((ng, 4, 2, 3, 8, 128), F32),
             pltpu.VMEM((2, nd, 3, 8, 128), F32),
             dma((database.shape[1] // BLOCK,)),
-            dma((2 * nd,)),
-            dma((2 * nd,)),
-            dma((ng, nd)),
-            dma((ng, nd)),
+            pltpu.SemaphoreType.REGULAR,
+            dma((2,)),
+            dma((2,)),
+            dma((ng,)),
+            dma((ng,)),
             dma((ng, 8)),
-            dma((2, nd)),
+            dma((2,)),
         ],
         compiler_params=pltpu.CompilerParams(
             collective_id=0, has_side_effects=True, vmem_limit_bytes=64_000_000),

time: 57.3 us -> 51.7 us (0.902)
  Pallas kernels: 55.8 us -> 50.2 us
    pallas_call x1, Pallas kernels: 55.8 us -> 50.2 us  [on_device(): pl.pallas_call(functools.partial(step_kernel, nq, nd), out_shape=jax.Shap...]
where the time goes in v3:
time: 51.7 us; the launch traced here: 51.5 us
  Pallas kernels  50.2 us (97%)
  local copies, waits for them, and re-layouts  1.31 us (3%)
    pallas_call x1, Pallas kernels, on_device(): pl.pallas_call(functools.partial(step_kernel, nq, nd), out_shape=jax.Shap...  50.2 us
    unnamed x1, local copies, waits for them, and re-layouts  1.31 us

profile of v3, /device:TPU:17, one launch (start us, length us, event | category | flops | bytes accessed | tf_op | source)
XLA Modules:
  0.0 51.5 jit_solution(3432288684357500078)
XLA Ops:
  0.0 50.2 %shard_map.55 = f32[1,3,8,128]{3,2,1,0:T(8,128)} custom-call(f32[1,3,8,128]{3,2,1,0:T(8,128)} %noisy_ref.1, bf16[432,16384]{1,0:T(8,128)(2,1)} %db_hbm.1, s32[1,4]{1,0:T(1,128)} %picked_ref.1, f32[16]{0:T(128)} %now_ref.1, f32[16]{0:T(128)} %next_ref.1), custom_call_target="tpu_custom_call" | custom-call | tf_op jit(solution)/shard_map/pallas_call | solution.py:310
  50.2 1.3 %copy.7 = f32[1,3,8,128]{3,2,1,0:T(8,128)} copy(f32[1,3,8,128]{3,2,1,0:T(8,128)} %shard_map.55) | data formatting | bytes 24576

commit v4 on v3

--- a/solution.py
+++ b/solution.py
@@ -20,7 +20,7 @@
 
 def step_kernel(nq, nd, noisy_ref, db_hbm, picked_ref, now_ref, next_ref, out_ref,
                 dbv, kt, sbuf0, sbuf1, wbuf0, wbuf1, wbuf2, qbuf, acc, sel, perm, ystack, zbuf, tally, gath, stat, pstage, precv,
-                dbsem, rowsem, gss, grs, sts, srs, pss, prs):
+                dbsem, gss, grs, sts, srs, pss, prs):
     ng = nd // 4
     keys = kt.shape[0]
     q = lax.axis_index("query")
@@ -49,6 +49,29 @@
     own_tile = noisy_ref[0].astype(BF16)
     gath[lo_me, g_me, 0] = own_tile
 
+    pl.semaphore_wait(barrier, nd + 1)
+
+    def column_copy():
+        return pltpu.make_async_remote_copy(
+            src_ref=gath.at[lo_me, g_me, 0], dst_ref=gath.at[lo_me, g_me, 1],
+            send_sem=gss.at[0], recv_sem=grs.at[0], device_id=(up, d), device_id_type=MESH)
+
+    def row_copy(half, o):
+        return pltpu.make_async_remote_copy(
+            src_ref=gath.at[lo_me, g_me, half], dst_ref=gath.at[lo_me, g_me, half],
+            send_sem=gss.at[1 + half], recv_sem=grs.at[1 + half],
+            device_id=(q, lax.rem(d + o, nd)), device_id_type=MESH)
+
+    def take(region, sem):
+        pltpu.make_async_copy(region, region, sem).wait()
+
+    def over_peers(step, first=1):
+        for o in range(first, nd):
+            step(o)
+
+    column_copy().start()
+    over_peers(lambda o: row_copy(0, o).start())
+
     def fill_sel(j, carry):
         lane = lax.broadcasted_iota(jnp.int32, (512, 128), 1)
         row = lax.broadcasted_iota(jnp.int32, (512, 128), 0)
@@ -67,29 +90,8 @@
 
     lax.fori_loop(0, 2, fill_perm, 0)
 
-    pl.semaphore_wait(barrier, nd + 1)
-    for row in (up, down):
-        pl.semaphore_signal(rowsem, inc=1, device_id=(row, d), device_id_type=MESH)
-
-    def tile_copy(half, o):
-        return pltpu.make_async_remote_copy(
-            src_ref=gath.at[lo_me, g_me, 0], dst_ref=gath.at[lo_me, g_me, half],
-            send_sem=gss.at[half], recv_sem=grs.at[half],
-            device_id=(up if half else q, lax.rem(d + o, nd)), device_id_type=MESH)
-
-    def take(region, sem):
-        pltpu.make_async_copy(region, region, sem).wait()
-
-    def tiles(half):
-        return tally.at[pl.ds(0, nd - 1 + half)]
-
-    def over_peers(step, first=1):
-        for o in range(first, nd):
-            step(o)
-
-    over_peers(lambda o: tile_copy(0, o).start())
-    pl.semaphore_wait(rowsem, 2)
-    over_peers(lambda o: tile_copy(1, o).start(), 0)
+    column_copy().wait_recv()
+    over_peers(lambda o: row_copy(1, o).start())
 
     for i in range(dbv.shape[0]):
         db_copy(i).wait()
@@ -136,7 +138,7 @@
         qbuf[g, pl.ds(432, 80), :] = extra.astype(BF16)
 
     for half in range(2):
-        take(tiles(half), grs.at[half])
+        take(tally, grs.at[1 + half])
 
     lanes = []
     for lo in range(4):
@@ -237,10 +239,11 @@
             pstage[g, lo, 0] = tile[:, :8]
             pstage[g, lo, 1] = tile[:, 8:]
         for lo in range(4):
+            pixel_send(g, lo, 1).start()
+        for lo in range(4):
             @pl.when(lo * ng + g != d)
             def _():
                 pixel_send(g, lo, 0).start()
-            pixel_send(g, lo, 1).start()
 
     neg = jnp.full((8, 256), -jnp.inf, F32)
     tops = {}
@@ -281,8 +284,9 @@
     for t in range(max(last - 2, 0) + 1, ng):
         phase(None, None, t)
 
+    column_copy().wait_send()
     for half in range(2):
-        take(tiles(half), gss.at[half])
+        take(tally, gss.at[1 + half])
     for g in range(ng):
         take(stat.at[g, pl.ds(0, nd - 1)], sts.at[g])
         for lo in range(4):
@@ -326,15 +330,14 @@
             pltpu.VMEM((288, 192), BF16),
             pltpu.VMEM((3, 192, ng * 128), BF16),
             pltpu.VMEM((576, 128), F32),
-            pltpu.VMEM((nd, 3, 8, 128), BF16),
+            pltpu.VMEM((nd - 1, 3, 8, 128), BF16),
             pltpu.VMEM((4, ng, 2, 3, 8, 128), BF16),
             pltpu.VMEM((ng, nd, 8, 128), F32),
             pltpu.VMEM((ng, 4, 2, 3, 8, 128), F32),
             pltpu.VMEM((2, nd, 3, 8, 128), F32),
             dma((database.shape[1] // BLOCK,)),
-            pltpu.SemaphoreType.REGULAR,
-            dma((2,)),
-            dma((2,)),
+            dma((3,)),
+            dma((3,)),
             dma((ng,)),
             dma((ng,)),
             dma((ng, 8)),

time: 51.7 us -> 50.2 us (0.971)
  Pallas kernels: 50.2 us -> 48.8 us
    pallas_call x1, Pallas kernels: 50.2 us -> 48.8 us  [on_device(): pl.pallas_call(functools.partial(step_kernel, nq, nd), out_shape=jax.Shap...]
where the time goes in v4:
time: 50.2 us; the launch traced here: 50.1 us
  Pallas kernels  48.8 us (97%)
  local copies, waits for them, and re-layouts  1.31 us (3%)
    pallas_call x1, Pallas kernels, on_device(): pl.pallas_call(functools.partial(step_kernel, nq, nd), out_shape=jax.Shap...  48.8 us
    unnamed x1, local copies, waits for them, and re-layouts  1.31 us

profile of v4, /device:TPU:17, one launch (start us, length us, event | category | flops | bytes accessed | tf_op | source)
XLA Modules:
  0.0 50.1 jit_solution(8458248800062388849)
XLA Ops:
  0.0 48.8 %shard_map.55 = f32[1,3,8,128]{3,2,1,0:T(8,128)} custom-call(f32[1,3,8,128]{3,2,1,0:T(8,128)} %noisy_ref.1, bf16[432,16384]{1,0:T(8,128)(2,1)} %db_hbm.1, s32[1,4]{1,0:T(1,128)} %picked_ref.1, f32[16]{0:T(128)} %now_ref.1, f32[16]{0:T(128)} %next_ref.1), custom_call_target="tpu_custom_call" | custom-call | tf_op jit(solution)/shard_map/pallas_call | solution.py:314
  48.8 1.3 %copy.7 = f32[1,3,8,128]{3,2,1,0:T(8,128)} copy(f32[1,3,8,128]{3,2,1,0:T(8,128)} %shard_map.55) | data formatting | bytes 24576

commit v5 on v4

--- a/solution.py
+++ b/solution.py
@@ -79,7 +79,7 @@
         sel[:, pl.ds(pl.multiple_of(j * 128, 128), 128)] = jnp.where(row == want, 1.0, 0.0).astype(BF16)
         return carry
 
-    lax.fori_loop(0, 12, fill_sel, 0)
+    lax.fori_loop(0, 4, fill_sel, 0)
 
     def fill_perm(r, carry):
         row = lax.broadcasted_iota(jnp.int32, (144, 192), 0)
@@ -137,6 +137,13 @@
         extra = jnp.where(row < 3, high, jnp.where(row < 5, mid, jnp.where(row == 5, low, 0.0)))
         qbuf[g, pl.ds(432, 80), :] = extra.astype(BF16)
 
+    def scale_of(g):
+        a = per_lane(now_ref, g, 1)
+        return LOG2E * jnp.sqrt(a) / (1.0 - a)
+
+    scales = [scale_of(g) for g in range(ng)]
+    acc[...] = jnp.zeros(acc.shape, F32)
+
     for half in range(2):
         take(tally, grs.at[1 + half])
 
@@ -145,14 +152,19 @@
         both = jnp.concatenate([gath[lo, :, 0].astype(F32), gath[lo, :, 1].astype(F32)], axis=2)
         lanes.append(both.reshape(ng * 48, 128))
     rows = jnp.concatenate(lanes, axis=1).astype(BF16)
-    for pair in range(6):
-        y = jnp.dot(rows, sel[:, pair * 256:(pair + 1) * 256], preferred_element_type=F32).astype(BF16)
-        for g in range(ng):
-            for c in range(3):
-                for k in range(2):
-                    j = 2 * pair + k
-                    ystack[c, j * 16:(j + 1) * 16, g * 128:(g + 1) * 128] = (
-                        y[(g * 3 + c) * 16:(g * 3 + c + 1) * 16, k * 128:(k + 1) * 128])
+    spread = jnp.dot(rows, sel[...], preferred_element_type=F32)
+    place = lax.broadcasted_iota(jnp.int32, (ng * 48, 128), 1) % 32
+    for k in range(4):
+        first_columns = spread[:, k * 128:(k + 1) * 128]
+        for shift in range(3):
+            y = first_columns
+            if shift:
+                y = jnp.where(place < 32 - shift, pltpu.roll(y, 128 - shift, 1), pltpu.roll(y, 32 - shift, 1))
+            y = y.astype(BF16)
+            j = 4 * shift + k
+            for g in range(ng):
+                for c in range(3):
+                    ystack[c, j * 16:(j + 1) * 16, g * 128:(g + 1) * 128] = y[(g * 3 + c) * 16:(g * 3 + c + 1) * 16, :]
     for c in range(3):
         placed = jnp.dot(perm[...], ystack[c], preferred_element_type=F32).astype(BF16)
         for g in range(ng):
@@ -182,10 +194,6 @@
     def gather_keys(g, slot, inside, start, size):
         cols = dbv[picked_ref[0, slot], :, inside:inside + size]
         acc[g] += jnp.dot(cols, wbufs[g % 3][pl.ds(start, size), :], preferred_element_type=F32)
-
-    def scale_of(g):
-        a = per_lane(now_ref, g, 1)
-        return LOG2E * jnp.sqrt(a) / (1.0 - a)
 
     def stat_send(g, o):
         return pltpu.make_async_remote_copy(
@@ -232,7 +240,7 @@
         high = flat.astype(BF16)
         low = (flat - high.astype(F32)).astype(BF16)
         both = jnp.concatenate([high, low], axis=0)
-        pix = lax.dot_general(both, sel[:, :512], (((1,), (1,)), ((), ())), preferred_element_type=F32)
+        pix = lax.dot_general(both, sel[...], (((1,), (1,)), ((), ())), preferred_element_type=F32)
         pix = pix[:48] + pix[48:]
         for lo in range(4):
             tile = pix[:, lo * 128:(lo + 1) * 128].reshape(3, 16, 128)
@@ -247,14 +255,11 @@
 
     neg = jnp.full((8, 256), -jnp.inf, F32)
     tops = {}
-    scales = {}
     def phase(first=None, second=None, third=None):
-        size = SUB // 2 if second is not None and (first is None or third is None) else SUB
-
-        if second is not None:
-            scales[second] = scale_of(second)
-        if third is not None:
-            acc[third] = jnp.zeros((432, 256), F32)
+        if second is not None and (first is None or third is None):
+            size = SUB // 2
+        else:
+            size = SUB if third is not None else 2 * SUB
 
         def body(i, carry):
             best, total = carry
@@ -326,7 +331,7 @@
             pltpu.VMEM((keys, 256), BF16),
             pltpu.VMEM((ng, 512, 256), BF16),
             pltpu.VMEM((ng, 432, 256), F32),
-            pltpu.VMEM((512, 1536), BF16),
+            pltpu.VMEM((512, 512), BF16),
             pltpu.VMEM((288, 192), BF16),
             pltpu.VMEM((3, 192, ng * 128), BF16),
             pltpu.VMEM((576, 128), F32),

time: 50.2 us -> 50 us (level)
  no operation moved by 1% of the time
where the time goes in v5:
time: 50 us; the launch traced here: 49.8 us
  Pallas kernels  48.5 us (97%)
  local copies, waits for them, and re-layouts  1.31 us (3%)
    pallas_call x1, Pallas kernels, on_device(): pl.pallas_call(functools.partial(step_kernel, nq, nd), out_shape=jax.Shap...  48.5 us
    unnamed x1, local copies, waits for them, and re-layouts  1.31 us

profile of v5, /device:TPU:17, one launch (start us, length us, event | category | flops | bytes accessed | tf_op | source)
XLA Modules:
  0.0 49.8 jit_solution(3618959146671481092)
XLA Ops:
  0.0 48.5 %shard_map.55 = f32[1,3,8,128]{3,2,1,0:T(8,128)} custom-call(f32[1,3,8,128]{3,2,1,0:T(8,128)} %noisy_ref.1, bf16[432,16384]{1,0:T(8,128)(2,1)} %db_hbm.1, s32[1,4]{1,0:T(1,128)} %picked_ref.1, f32[16]{0:T(128)} %now_ref.1, f32[16]{0:T(128)} %next_ref.1), custom_call_target="tpu_custom_call" | custom-call | tf_op jit(solution)/shard_map/pallas_call | solution.py:319
  48.5 1.3 %copy.7 = f32[1,3,8,128]{3,2,1,0:T(8,128)} copy(f32[1,3,8,128]{3,2,1,0:T(8,128)} %shard_map.55) | data formatting | bytes 24576
